TPU v7x, 32 devices: a whole 2x2x4 slice. The times are simulated.
32 devices in a mesh: ctx: 8 (over z, x), ch: 4 (over y, core).
Axes of the slice: x: 2, y: 2, z: 4, core: 2. Of those that a mesh axis runs over, the one named last changes fastest.
Arguments:
- query_input: bfloat16 [4096, 4096], P('ch', 'ctx'), may hold values from -6 to 6
- key_input: bfloat16 [4096, 4096], P('ch', 'ctx'), may hold values from -6 to 6
- value_input: bfloat16 [4096, 4096], P('ch', 'ctx'), may hold values from -6 to 6
- decay_rate: float32 [8, 16], P('ch'), may hold values from 0 to 1, as said below
- residue: float32 [8, 16], P('ch'), may hold values from -1 to 1
- doc_ends: int32 [4], replicated, may hold values from 1 to 4096, as said below
- out_weight: bfloat16 [4096, 4096], P(None, 'ch'), may hold values from -0.09375 to 0.09375
- out_cotangent: bfloat16 [4096, 4096], P('ctx', 'ch'), may hold values from -6 to 6
Outputs:
- query_grad: bfloat16 [4096, 4096], P('ch', 'ctx')
- key_grad: bfloat16 [4096, 4096], P('ch', 'ctx')
- value_grad: bfloat16 [4096, 4096], P('ch', 'ctx')
- weight_grad: float32 [4096, 4096], P('ctx', 'ch')
Inputs may be any that keep to these rules, and one draw needn't show every extreme that they name: `doc_ends`: strictly increasing; the last entry equals 4096. `decay_rate`: positive.
All inputs are finite; a program needn't handle non-finite values.
Results may differ from a plain program's by a relative error of at most 0.0029.
Values may be sent and summed in bfloat16 or wider, within the bound.
A program may use at most 128 MiB of HBM per device.

v0:
```python
import math
import jax
import jax.numpy as jnp
from jax import lax
from jax.sharding import PartitionSpec as P

HIGH = lax.Precision.HIGH
TILE = 128


def doc_of(doc_ends, positions):
    return jnp.sum((doc_ends[None, :] <= positions[:, None]).astype(jnp.int32), axis=1)


def local_kernel(decay_rate, residue, doc_ids, length):
    groups = decay_rate.shape[0]
    place = jnp.arange(length, dtype=jnp.float32)
    narrow = jnp.arange(TILE, dtype=jnp.float32)
    half = 0.5 * TILE
    rising = jnp.exp(-decay_rate[:, None, :] * (place - half)[None, :, None]) * residue[:, None, :]
    falling = jnp.exp(decay_rate[:, None, :] * (narrow - half)[None, :, None])
    strip = jnp.einsum("gtn,gsn->gts", rising, falling, precision=lax.Precision.HIGHEST)
    columns = []
    for start in range(0, length, TILE):
        top = jnp.zeros((groups, start, TILE), jnp.float32)
        columns.append(jnp.concatenate([top, strip[:, : length - start]], axis=1))
    kernel = jnp.concatenate(columns, axis=2)
    offsets = jnp.arange(length, dtype=jnp.int32)
    causal = (offsets[:, None] >= offsets[None, :]) & (doc_ids[:, None] == doc_ids[None, :])
    return jnp.where(causal[None], kernel, 0.0)


def exchange_rows(gated, n_ctx, n_ch):
    rows, length = gated.shape
    mine = rows * n_ch // n_ctx
    pieces = gated.reshape(n_ctx // n_ch, n_ch, mine // n_ch, length)
    pieces = lax.all_to_all(pieces, "ch", split_axis=1, concat_axis=0, tiled=True)
    pieces = pieces.reshape(n_ctx, mine // n_ch, length)
    pieces = lax.all_to_all(pieces, "ctx", split_axis=0, concat_axis=0, tiled=True)
    pieces = pieces.transpose(1, 0, 2).reshape(mine // n_ch, n_ctx * length)
    return lax.all_gather(pieces, "ch", axis=0, tiled=True)


def local(
    query_input, key_input, value_input, decay_rate, residue, doc_ends, out_weight, out_cotangent
):
    rows_here, length = query_input.shape
    n_ctx, n_ch = (lax.axis_size("ctx"), lax.axis_size("ch"))
    groups = decay_rate.shape[0]
    group_rows = rows_here // groups
    me = lax.axis_index("ctx")
    offsets = jnp.arange(length, dtype=jnp.int32)
    place = offsets.astype(jnp.float32)
    doc_ids = doc_of(doc_ends, me * length + offsets)
    blocks = jnp.arange(n_ctx, dtype=jnp.int32)
    last_ids = doc_of(doc_ends, (blocks + 1) * length - 1)
    previous = jnp.where(me > 0, jnp.sum((doc_ends <= me * length - 1).astype(jnp.int32)), -1)
    last = doc_ids[-1]
    cotangent_all = lax.all_gather(out_cotangent, "ctx", axis=0, tiled=True)
    alive_mask = (doc_ids == previous).astype(jnp.float32)
    tail_mask = (doc_ids == last).astype(jnp.float32)
    rate = decay_rate[:, :, None]
    carry_in_map = residue[:, :, None] * jnp.exp(-rate * (place + 1.0)) * alive_mask
    carry_out_map = jnp.exp(-rate * (length - 1.0 - place)) * tail_mask
    back_out_map = jnp.exp(-rate * place) * alive_mask
    back_in_map = residue[:, :, None] * jnp.exp(-rate * (length - place)) * tail_mask
    steps_ahead = me - 1 - blocks
    joined_ahead = (steps_ahead >= 0) & (last_ids == previous)
    ahead_weight = jnp.where(
        joined_ahead[:, None, None],
        jnp.exp(
            -decay_rate[None]
            * (length * jnp.maximum(steps_ahead, 0)).astype(jnp.float32)[:, None, None]
        ),
        0.0,
    )
    steps_back = blocks - 1 - me
    before_ids = jnp.concatenate([jnp.full((1,), -1, jnp.int32), last_ids[:-1]])
    joined_back = (steps_back >= 0) & (before_ids == last)
    back_weight = jnp.where(
        joined_back[:, None, None],
        jnp.exp(
            -decay_rate[None]
            * (length * jnp.maximum(steps_back, 0)).astype(jnp.float32)[:, None, None]
        ),
        0.0,
    )
    key_f = key_input.astype(jnp.float32)
    value_f = value_input.astype(jnp.float32)
    query_f = query_input.astype(jnp.float32)
    mixed = (key_f * value_f).reshape(groups, group_rows, length)
    forward_part = jnp.einsum("gnl,gcl->gnc", carry_out_map, mixed, precision=HIGH)
    forward_all = lax.all_gather(forward_part, "ctx", axis=0)
    entering = jnp.sum(ahead_weight[..., None] * forward_all, axis=0)
    partial_grad = lax.dot_general(
        out_weight, out_cotangent, (((1,), (1,)), ((), ())), preferred_element_type=jnp.float32
    )
    output_grad = lax.psum_scatter(partial_grad, "ch", scatter_dimension=0, tiled=True)
    kernel = local_kernel(decay_rate, residue, doc_ids, length)
    filtered = jnp.einsum("gcs,gts->gct", mixed, kernel, precision=HIGH)
    filtered = filtered + jnp.einsum("gnc,gnt->gct", entering, carry_in_map, precision=HIGH)
    filtered = filtered.reshape(rows_here, length)
    gated = (query_f * filtered).astype(jnp.bfloat16)
    gated_rows = exchange_rows(gated, n_ctx, n_ch)
    signal = (output_grad * query_f).reshape(groups, group_rows, length)
    backward_part = jnp.einsum("gnl,gcl->gnc", back_out_map, signal, precision=HIGH)
    backward_all = lax.all_gather(backward_part, "ctx", axis=0)
    query_grad = (output_grad * filtered).astype(jnp.bfloat16)
    spread = jnp.einsum("gct,gts->gcs", signal, kernel, precision=HIGH)
    returning = jnp.sum(back_weight[..., None] * backward_all, axis=0)
    spread = spread + jnp.einsum("gnc,gns->gcs", returning, back_in_map, precision=HIGH)
    spread = spread.reshape(rows_here, length)
    key_grad = (spread * value_f).astype(jnp.bfloat16)
    value_grad = (spread * key_f).astype(jnp.bfloat16)
    norm_factor = 1.0 / math.sqrt(length * n_ctx)
    weight_grad = (
        jnp.dot(gated_rows, cotangent_all, preferred_element_type=jnp.float32) * norm_factor
    )
    return (query_grad, key_grad, value_grad, weight_grad)


def solution(mesh):
    return jax.shard_map(
        local,
        mesh=mesh,
        in_specs=(
            P("ch", "ctx"),
            P("ch", "ctx"),
            P("ch", "ctx"),
            P("ch", None),
            P("ch", None),
            P(),
            P(None, "ch"),
            P("ctx", "ch"),
        ),
        out_specs=(P("ch", "ctx"), P("ch", "ctx"), P("ch", "ctx"), P("ctx", "ch")),
        check_vma=False,
    )
```

profile of v0, /device:TPU:0, one launch (start us, length us, event | category | flops | bytes accessed | tf_op | source)
XLA Modules:
  0.0 227.6 jit_solution(17652264326971221755)
XLA Ops:
  8.0 11.4 %fusion.67 = f32[4096,512]{1,0:T(8,128)} fusion(bf16[4096,1024]{1,0:T(8,128)(2,1)} %param.14, bf16[512,1024]{1,0:T(8,128)(2,1)} %param.15), kind=kOutput, calls=%fused_computation.103 | convolution fusion | flops 4294967296 | bytes 17825792 | tf_op jit(solution)/shard_map/dot_general | solution.py:95
  19.6 0.5 all-gather.7.cloned.1.call-update
  20.2 0.7 fusion.28
  21.2 0.6 slice.18
  21.8 0.6 fusion.56
  23.2 0.7 compare_and_fusion
  23.9 0.6 compare_convert_fusion
  24.7 0.3 convert_multiply_fusion.3
  25.0 0.9 fusion.24
  25.9 35.0 %all-gather = f32[16,16,512]{2,1,0:T(8,128)S(1)} all-gather(f32[2,16,512]{2,1,0:T(8,128)S(1)} %fusion.24), channel_id=2, replica_groups=mesh['ctx'=8,'ch'=4] {'ctx'}, dimensions={0}, use_global_device_ids=true | all-gather | bytes 589824 | tf_op jit(solution)/shard_map/all_gather | solution.py:93
  61.3 1.9 fusion.10
  63.2 2.4 %convolution_add_fusion.1 = f32[2,512,512]{2,1,0:T(8,128)} fusion(f32[2,512,512]{2,1,0:T(8,128)S(1)} %fusion.10, f32[2,16,512]{2,1,0:T(8,128)S(1)} %multiply_reduce_fusion.1, f32[512]{0:T(512)S(1)} %get-tuple-element.9, f32[512]{0:T(512)S(1)} %fusion.54, f32[2,16]{1,0:T(2,128)S(1)} %copy-done.15, f32[2,16]{1,0:T(2,128)S(1)} %neg.5), kind=kOutput, calls=%fused_computation.22 | convolution fusion | flops 50905088 | bytes 4264192 | tf_op jit(solution)/shard_map/gnc,gnt->gct/dot_general | solution.py:101
  65.6 28.5 %reduce-scatter.2.cloned.1.call-done = f32[1024,512]{1,0:T(8,128)} async-done(((f32[4096,512]{1,0:T(8,128)}), f32[1024,512]{1,0:T(8,128)}) %reduce-scatter.2.cloned.1.call-update) | async-done | bytes 2097168 | tf_op jit(solution)/shard_map/reduce_scatter | solution.py:98
  94.1 3.9 %fusion.2 = (bf16[1024,512]{1,0:T(8,128)(2,1)S(1)}, bf16[1024,512]{1,0:T(8,128)(2,1)}, f32[1024,512]{1,0:T(8,128)S(1)}) fusion(bf16[1024,512]{1,0:T(8,128)(2,1)S(1)} %copy-done.6, f32[2,512,512]{2,1,0:T(8,128)} %convolution_add_fusion.1, f32[1024,512]{1,0:T(8,128)} %reduce-scatter.2.cloned.1.call-done), kind=kLoop, calls=%fused_computation.11 | loop fusion | flops 3145728 | bytes 9437184 | tf_op jit(solution)/shard_map/convert_element_type | solution.py:103
  98.1 16.9 %all_to_all.20 = bf16[2,4,128,512]{3,2,0,1:T(8,128)(2,1)S(1)} all-to-all(bf16[2,4,128,512]{3,2,0,1:T(8,128)(2,1)S(1)} %copy.24), channel_id=1, replica_groups=mesh['ctx'=8,'ch'=4] {'ch'}, dimensions={1} | all-to-all | bytes 2097152 | tf_op jit(solution)/shard_map/all_to_all | solution.py:37
  115.0 54.5 %all_to_all.21 = bf16[8,128,512]{2,1,0:T(8,128)(2,1)S(1)} all-to-all(bf16[8,128,512]{2,1,0:T(8,128)(2,1)S(1)} %bitcast.38), channel_id=1, replica_groups=mesh['ctx'=8,'ch'=4] {'ctx'}, dimensions={0} | all-to-all | bytes 2097152 | tf_op jit(solution)/shard_map/all_to_all | solution.py:39
  169.5 1.3 copy.25
  170.9 1.7 fusion.16
  172.6 31.6 %all-gather.1 = f32[16,16,512]{2,1,0:T(8,128)S(1)} all-gather(f32[2,16,512]{2,1,0:T(8,128)S(1)} %fusion.16), channel_id=3, replica_groups=mesh['ctx'=8,'ch'=4] {'ctx'}, dimensions={0}, use_global_device_ids=true | all-gather | bytes 589824 | tf_op jit(solution)/shard_map/all_gather | solution.py:107
  204.4 1.9 fusion.8
  206.3 1.0 convolution_add_fusion
  207.5 0.3 copy-done.3
  207.8 1.9 fusion
  209.7 10.5 %convolution_multiply_fusion = f32[512,1024]{1,0:T(8,128)} fusion(bf16[512,4096]{0,1:T(8,128)(2,1)} %all-gather.5.cloned.1.call-done, bf16[4096,1024]{1,0:T(8,128)(2,1)} %all-gather.7.cloned.1.call-done), kind=kOutput, calls=%fused_computation.23 | convolution fusion | flops 4295491584 | bytes 14680064 | tf_op jit(solution)/shard_map/dot_general | solution.py:117
  (64 shorter events, 1.3 us)
Async XLA Ops:
  8.0 86.1 %reduce-scatter.2.cloned.1.call-start = ((), (), s32[]{:S(2)}) async-start(), calls=%async_computation.3 | async-start | bytes 10485760 | tf_op jit(solution)/shard_map/reduce_scatter | solution.py:98
  19.5 0.7 copy-start.17
  19.5 0.7 copy-start.14
  19.5 1.6 copy-start.18
  19.5 5.2 %copy-start = (bf16[1024,512]{1,0:T(8,128)(2,1)S(1)}, bf16[1024,512]{1,0:T(8,128)(2,1)}, u32[]{:S(2)}) copy-start(bf16[1024,512]{1,0:T(8,128)(2,1)} %param.10) | copy-start | bytes 3145732
  19.5 5.2 %copy-start.2 = (bf16[1024,512]{1,0:T(8,128)(2,1)S(1)}, bf16[1024,512]{1,0:T(8,128)(2,1)}, u32[]{:S(2)}) copy-start(bf16[1024,512]{1,0:T(8,128)(2,1)} %param.9) | copy-start | bytes 3145732
  19.5 190.1 %all-gather.7.cloned.1.call-start = ((), (), s32[]{:S(2)}) async-start(), calls=%async_computation.5 | async-start | bytes 9437184 | tf_op jit(solution)/shard_map/all_gather | solution.py:59
  20.1 189.6 %all-gather.5.cloned.1.call-start = ((), (), s32[]{:S(2)}) async-start(), calls=%async_computation.4 | async-start | bytes 5242880 | tf_op jit(solution)/shard_map/all_gather | solution.py:41
  20.9 40.3 %copy-start.4 = (f32[2,512,128]{1,2,0:T(8,128)}, f32[2,512,128]{1,2,0:T(8,128)S(1)}, u32[]{:S(2)}) copy-start(f32[2,512,128]{1,2,0:T(8,128)S(1)} %fusion.28) | copy-start | bytes 1572868
  21.0 40.3 %copy-start.11 = (f32[2,128,128]{1,2,0:T(8,128)}, f32[2,128,128]{1,2,0:T(8,128)S(1)}, u32[]{:S(2)}) copy-start(f32[2,128,128]{1,2,0:T(8,128)S(1)} %slice.22) | copy-start | bytes 393220
  21.0 40.3 %copy-start.7 = (f32[2,256,128]{1,2,0:T(8,128)}, f32[2,256,128]{1,2,0:T(8,128)S(1)}, u32[]{:S(2)}) copy-start(f32[2,256,128]{1,2,0:T(8,128)S(1)} %slice.21) | copy-start | bytes 786436
  24.6 38.6 %copy-start.13 = (f32[512]{0:T(512)}, f32[512]{0:T(512)S(1)}, u32[]{:S(2)}) copy-start(f32[512]{0:T(512)S(1)} %get-tuple-element.9) | copy-start | bytes 6148
  61.3 1.9 copy-start.9
  61.3 1.9 copy-start.15
  63.2 30.9 %copy-start.6 = (bf16[1024,512]{1,0:T(8,128)(2,1)S(1)}, bf16[1024,512]{1,0:T(8,128)(2,1)}, u32[]{:S(2)}) copy-start(bf16[1024,512]{1,0:T(8,128)(2,1)} %param.8) | copy-start | bytes 3145732
  170.8 33.5 %copy-start.5 = (f32[2,512,128]{1,2,0:T(8,128)S(1)}, f32[2,512,128]{1,2,0:T(8,128)}, u32[]{:S(2)}) copy-start(f32[2,512,128]{1,2,0:T(8,128)} %copy-done.4) | copy-start | bytes 1572868
  170.8 33.5 %copy-start.8 = (f32[2,256,128]{1,2,0:T(8,128)S(1)}, f32[2,256,128]{1,2,0:T(8,128)}, u32[]{:S(2)}) copy-start(f32[2,256,128]{1,2,0:T(8,128)} %copy-done.7) | copy-start | bytes 786436
  170.8 33.5 %copy-start.12 = (f32[2,128,128]{1,2,0:T(8,128)S(1)}, f32[2,128,128]{1,2,0:T(8,128)}, u32[]{:S(2)}) copy-start(f32[2,128,128]{1,2,0:T(8,128)} %copy-done.11) | copy-start | bytes 393220
  170.8 33.5 %copy-start.10 = (pred[512,512]{0,1:T(8,128)(4,1)S(1)}, pred[512,512]{0,1:T(8,128)(4,1)}, u32[]{:S(2)}) copy-start(pred[512,512]{0,1:T(8,128)(4,1)} %copy-done.9) | copy-start | bytes 786436
  204.3 1.9 copy-start.16
  206.3 1.2 copy-start.1
  206.3 1.5 copy-start.3
Sparse Core Ops, SparseCore 0:
  19.6 74.4 reduce-scatter.1
Sparse Core Ops, SparseCore 1:
  22.4 151.2 all-gather.6
  175.7 33.9 all-gather.4
where the time goes:
time: 228 us
  blocking collectives  138 us (61%)
  matrix products  32.5 us (14%)
  waiting for transfers between devices  29.1 us (13%)
  between operations  16.6 us (7%)
  other arithmetic  8.81 us (4%)
  local copies, waits for them, and re-layouts  2.62 us (1%)
    all_to_all x1, blocking collectives, exchange_rows(): lax.all_to_all(pieces, 'ctx', split_axis=0, concat_axis=0, tiled=True)  54.5 us
    all_gather x1, blocking collectives, local(): forward_all = lax.all_gather(forward_part, 'ctx', axis=0)  35 us
    all_gather x1, blocking collectives, local(): backward_all = lax.all_gather(backward_part, 'ctx', axis=0)  31.6 us
    reduce_scatter x1, waiting for transfers between devices, local(): lax.psum_scatter(partial_grad, 'ch', scatter_dimension=0, tiled=True)  28.5 us
    all_to_all x1, blocking collectives, exchange_rows(): lax.all_to_all(pieces, 'ch', split_axis=1, concat_axis=0, tiled=True)  16.9 us
    dot_general x1, matrix products, local(): lax.dot_general(out_weight, out_cotangent, (((1,), (1,)), ((), ())), pref...  11.4 us
    dot_general x1, matrix products, local(): jnp.dot(gated_rows, cotangent_all, preferred_element_type=jnp.float32)  10.5 us
  transfers between devices with their start and end apart: 3, of which 1 were waited for; matrix products, arithmetic and copies ran while one was open for 9% of the time, Pallas kernels for 0%

commit v1 on v0

--- a/solution.py
+++ b/solution.py
@@ -6,6 +6,28 @@
 
 HIGH = lax.Precision.HIGH
 TILE = 128
+
+
+def cut_along(x, dim, peers):
+    before, after = (x.shape[:dim], x.shape[dim + 1 :])
+    return jnp.moveaxis(x.reshape(*before, peers, -1, *after), dim, 0)
+
+
+def joined_along(tiles, dim):
+    shape = list(tiles.shape[1:])
+    shape[dim] *= tiles.shape[0]
+    return jnp.moveaxis(tiles, 0, dim).reshape(shape)
+
+
+def exchange_in_pairs(x, axis, split_dim, concat_dim):
+    devices, index = (lax.axis_size(axis), lax.axis_index(axis))
+    pieces = cut_along(x, split_dim, devices)
+    outs = [pieces[index]]
+    for step in range(1, devices):
+        sent = pieces[index ^ step]
+        outs.append(lax.ppermute(sent, axis, [(i, i ^ step) for i in range(devices)]))
+    pieces = jnp.stack(outs)[index ^ jnp.arange(devices)]
+    return joined_along(pieces, concat_dim)
 
 
 def doc_of(doc_ends, positions):
@@ -34,7 +56,7 @@
     rows, length = gated.shape
     mine = rows * n_ch // n_ctx
     pieces = gated.reshape(n_ctx // n_ch, n_ch, mine // n_ch, length)
-    pieces = lax.all_to_all(pieces, "ch", split_axis=1, concat_axis=0, tiled=True)
+    pieces = exchange_in_pairs(pieces, "ch", 1, 0)
     pieces = pieces.reshape(n_ctx, mine // n_ch, length)
     pieces = lax.all_to_all(pieces, "ctx", split_axis=0, concat_axis=0, tiled=True)
     pieces = pieces.transpose(1, 0, 2).reshape(mine // n_ch, n_ctx * length)

time: 228 us -> 227 us (level)
  blocking collectives: 138 us -> 120 us
  waiting for transfers between devices: 29.1 us -> 41.4 us
    all_to_all x1 -> x0, blocking collectives: 16.9 us -> none  [exchange_rows(): lax.all_to_all(pieces, 'ch', split_axis=1, concat_axis=0, tiled=True)]
    ppermute x0 -> x3, waiting for transfers between devices: none -> 11.7 us  [exchange_in_pairs(): lax.ppermute(sent, axis, [(i, i ^ step) for i in range(devices)])]
  transfers between devices with their start and end apart: 3 -> 6, of which waited for: 1 -> 4; matrix products, arithmetic and copies ran while one was open for 9% -> 11% of each run, Pallas kernels for 0% -> 0%
where the time goes in v1:
time: 227 us
  blocking collectives  120 us (53%)
  waiting for transfers between devices  41.4 us (18%)
  matrix products  32.4 us (14%)
  between operations  16.6 us (7%)
  other arithmetic  9.61 us (4%)
  local copies, waits for them, and re-layouts  4.63 us (2%)
    all_to_all x1, blocking collectives, exchange_rows(): lax.all_to_all(pieces, 'ctx', split_axis=0, concat_axis=0, tiled=True)  53.7 us
    all_gather x1, blocking collectives, local(): forward_all = lax.all_gather(forward_part, 'ctx', axis=0)  34.8 us
    all_gather x1, blocking collectives, local(): backward_all = lax.all_gather(backward_part, 'ctx', axis=0)  31.5 us
    reduce_scatter x1, waiting for transfers between devices, local(): lax.psum_scatter(partial_grad, 'ch', scatter_dimension=0, tiled=True)  28.5 us
    ppermute x3, waiting for transfers between devices, exchange_in_pairs(): lax.ppermute(sent, axis, [(i, i ^ step) for i in range(devices)])  11.7 us
    dot_general x1, matrix products, local(): lax.dot_general(out_weight, out_cotangent, (((1,), (1,)), ((), ())), pref...  11.4 us
    dot_general x1, matrix products, local(): jnp.dot(gated_rows, cotangent_all, preferred_element_type=jnp.float32)  10.5 us
  transfers between devices with their start and end apart: 6, of which 4 were waited for; matrix products, arithmetic and copies ran while one was open for 11% of the time, Pallas kernels for 0%

profile of v1, /device:TPU:0, one launch (start us, length us, event | category | flops | bytes accessed | tf_op | source)
XLA Modules:
  0.0 226.9 jit_solution(4695350531853228166)
XLA Ops:
  8.0 11.4 %fusion.68 = f32[4096,512]{1,0:T(8,128)} fusion(bf16[4096,1024]{1,0:T(8,128)(2,1)} %param.14, bf16[512,1024]{1,0:T(8,128)(2,1)} %param.15), kind=kOutput, calls=%fused_computation.112 | convolution fusion | flops 4294967296 | bytes 17825792 | tf_op jit(solution)/shard_map/dot_general | solution.py:117
  20.2 0.7 fusion.28
  21.8 0.6 fusion.56
  23.2 0.7 compare_and_fusion
  23.9 0.6 compare_convert_fusion
  25.0 1.0 fusion.24
  26.0 34.8 %all-gather = f32[16,16,512]{2,1,0:T(8,128)S(1)} all-gather(f32[2,16,512]{2,1,0:T(8,128)S(1)} %fusion.24), channel_id=2, replica_groups=mesh['ctx'=8,'ch'=4] {'ctx'}, dimensions={0}, use_global_device_ids=true | all-gather | bytes 589824 | tf_op jit(solution)/shard_map/all_gather | solution.py:115
  61.2 1.9 fusion.10
  63.2 2.4 %convolution_add_fusion.1 = f32[2,512,512]{2,1,0:T(8,128)} fusion(f32[2,512,512]{2,1,0:T(8,128)S(1)} %fusion.10, f32[2,16,512]{2,1,0:T(8,128)S(1)} %multiply_reduce_fusion.1, f32[512]{0:T(512)S(1)} %get-tuple-element.13, f32[512]{0:T(512)S(1)} %fusion.54, f32[2,16]{1,0:T(2,128)S(1)} %copy-done.15, f32[2,16]{1,0:T(2,128)S(1)} %neg.5), kind=kOutput, calls=%fused_computation.23 | convolution fusion | flops 50905088 | bytes 4264192 | tf_op jit(solution)/shard_map/gnc,gnt->gct/dot_general | solution.py:123
  65.6 28.5 %reduce-scatter.2.cloned.1.call-done = f32[1024,512]{1,0:T(8,128)} async-done(((f32[4096,512]{1,0:T(8,128)}), f32[1024,512]{1,0:T(8,128)}) %reduce-scatter.2.cloned.1.call-update) | async-done | bytes 2097168 | tf_op jit(solution)/shard_map/reduce_scatter | solution.py:120
  94.1 4.0 %fusion.2 = (bf16[1024,512]{1,0:T(8,128)(2,1)S(1)}, bf16[1024,512]{1,0:T(8,128)(2,1)}, f32[1024,512]{1,0:T(8,128)S(1)}) fusion(bf16[1024,512]{1,0:T(8,128)(2,1)S(1)} %copy-done.6, f32[2,512,512]{2,1,0:T(8,128)} %convolution_add_fusion.1, f32[1024,512]{1,0:T(8,128)} %reduce-scatter.2.cloned.1.call-done), kind=kLoop, calls=%fused_computation.12 | loop fusion | flops 3145728 | bytes 9437184 | tf_op jit(solution)/shard_map/convert_element_type | solution.py:125
  98.2 1.4 collective-permute-start.1
  100.7 6.1 %collective-permute-done.2 = bf16[2,1,128,512]{3,2,0,1:T(8,128)(2,1)S(1)} collective-permute-done((bf16[2,1,128,512]{3,2,0,1:T(8,128)(2,1)S(1)}, bf16[2,1,128,512]{3,2,0,1:T(8,128)(2,1)S(1)}, u32[]{:S(2)}, u32[]{:S(2)}) %collective-permute-start.2) | collective-permute-done | bytes 262176 | tf_op jit(solution)/shard_map/ppermute | solution.py:28
  106.8 5.6 %collective-permute-done.1 = bf16[2,1,128,512]{3,2,0,1:T(8,128)(2,1)S(1)} collective-permute-done((bf16[2,1,128,512]{3,2,0,1:T(8,128)(2,1)S(1)}, bf16[2,1,128,512]{3,2,0,1:T(8,128)(2,1)S(1)}, u32[]{:S(2)}, u32[]{:S(2)}) %collective-permute-start.1) | collective-permute-done | bytes 262176 | tf_op jit(solution)/shard_map/ppermute | solution.py:28
  112.5 1.7 gather_fusion
  114.3 1.6 copy.24
  115.9 53.7 %all_to_all.5 = bf16[8,128,512]{1,2,0:T(8,128)(2,1)} all-to-all(bf16[8,128,512]{1,2,0:T(8,128)(2,1)S(1)} %copy.24), channel_id=1, replica_groups=mesh['ctx'=8,'ch'=4] {'ctx'}, dimensions={0} | all-to-all | bytes 2097152 | tf_op jit(solution)/shard_map/all_to_all | solution.py:61
  169.7 1.6 fusion.16
  171.3 31.5 %all-gather.1 = f32[16,16,512]{2,1,0:T(8,128)S(1)} all-gather(f32[2,16,512]{2,1,0:T(8,128)S(1)} %fusion.16), channel_id=3, replica_groups=mesh['ctx'=8,'ch'=4] {'ctx'}, dimensions={0}, use_global_device_ids=true | all-gather | bytes 589824 | tf_op jit(solution)/shard_map/all_gather | solution.py:129
  203.0 1.8 fusion.8
  204.9 1.0 convolution_add_fusion
  206.4 1.9 fusion
  208.3 0.7 all-gather.5.cloned.1.call-done
  209.0 10.5 %convolution_multiply_fusion = f32[512,1024]{1,0:T(8,128)} fusion(bf16[512,4096]{0,1:T(8,128)(2,1)} %all-gather.5.cloned.1.call-done, bf16[4096,1024]{1,0:T(8,128)(2,1)} %all-gather.7.cloned.1.call-done), kind=kOutput, calls=%fused_computation.24 | convolution fusion | flops 4295491584 | bytes 14680064 | tf_op jit(solution)/shard_map/dot_general | solution.py:139
  (73 shorter events, 4.3 us)
Async XLA Ops:
  8.0 86.1 %reduce-scatter.2.cloned.1.call-start = ((), (), s32[]{:S(2)}) async-start(), calls=%async_computation.2 | async-start | bytes 10485760 | tf_op jit(solution)/shard_map/reduce_scatter | solution.py:120
  19.5 0.7 copy-start.14
  19.5 1.6 copy-start.18
  19.5 5.2 %copy-start = (bf16[1024,512]{1,0:T(8,128)(2,1)S(1)}, bf16[1024,512]{1,0:T(8,128)(2,1)}, u32[]{:S(2)}) copy-start(bf16[1024,512]{1,0:T(8,128)(2,1)} %param.10) | copy-start | bytes 3145732
  19.5 5.2 %copy-start.2 = (bf16[1024,512]{1,0:T(8,128)(2,1)S(1)}, bf16[1024,512]{1,0:T(8,128)(2,1)}, u32[]{:S(2)}) copy-start(bf16[1024,512]{1,0:T(8,128)(2,1)} %param.9) | copy-start | bytes 3145732
  19.5 188.8 %all-gather.7.cloned.1.call-start = ((), (), s32[]{:S(2)}) async-start(), calls=%async_computation.4 | async-start | bytes 9437184 | tf_op jit(solution)/shard_map/all_gather | solution.py:81
  20.1 188.9 %all-gather.5.cloned.1.call-start = ((), (), s32[]{:S(2)}) async-start(), calls=%async_computation.3 | async-start | bytes 5242880 | tf_op jit(solution)/shard_map/all_gather | solution.py:63
  20.9 40.3 %copy-start.4 = (f32[2,512,128]{1,2,0:T(8,128)}, f32[2,512,128]{1,2,0:T(8,128)S(1)}, u32[]{:S(2)}) copy-start(f32[2,512,128]{1,2,0:T(8,128)S(1)} %fusion.28) | copy-start | bytes 1572868
  21.0 40.2 %copy-start.11 = (f32[2,128,128]{1,2,0:T(8,128)}, f32[2,128,128]{1,2,0:T(8,128)S(1)}, u32[]{:S(2)}) copy-start(f32[2,128,128]{1,2,0:T(8,128)S(1)} %slice.24) | copy-start | bytes 393220
  21.0 40.2 %copy-start.7 = (f32[2,256,128]{1,2,0:T(8,128)}, f32[2,256,128]{1,2,0:T(8,128)S(1)}, u32[]{:S(2)}) copy-start(f32[2,256,128]{1,2,0:T(8,128)S(1)} %slice.23) | copy-start | bytes 786436
  24.6 38.6 %copy-start.13 = (f32[512]{0:T(512)}, f32[512]{0:T(512)S(1)}, u32[]{:S(2)}) copy-start(f32[512]{0:T(512)S(1)} %get-tuple-element.13) | copy-start | bytes 6148
  61.2 1.9 copy-start.9
  61.2 2.0 copy-start.15
  63.2 30.9 %copy-start.6 = (bf16[1024,512]{1,0:T(8,128)(2,1)S(1)}, bf16[1024,512]{1,0:T(8,128)(2,1)}, u32[]{:S(2)}) copy-start(bf16[1024,512]{1,0:T(8,128)(2,1)} %param.8) | copy-start | bytes 3145732
  98.1 8.7 %collective-permute-start.2 = (bf16[2,1,128,512]{3,2,0,1:T(8,128)(2,1)S(1)}, bf16[2,1,128,512]{3,2,0,1:T(8,128)(2,1)S(1)}, u32[]{:S(2)}, u32[]{:S(2)}) collective-permute-start(bf16[2,1,128,512]{3,2,0,1:T(8,128)(2,1)S(1)} %get-tuple-element.10), channel_id=1, source_target_pairs={{0,3},{1,2},{2,1},{3,0},{4,7},{5,6},{6,5},{7,4},{8,11},{9,10},{10,... | collective-permute-start | bytes 786440 | tf_op jit(solution)/shard_map/ppermute | solution.py:28
  98.2 14.2 %collective-permute-start.1 = (bf16[2,1,128,512]{3,2,0,1:T(8,128)(2,1)S(1)}, bf16[2,1,128,512]{3,2,0,1:T(8,128)(2,1)S(1)}, u32[]{:S(2)}, u32[]{:S(2)}) collective-permute-start(bf16[2,1,128,512]{3,2,0,1:T(8,128)(2,1)S(1)} %get-tuple-element.11), channel_id=1, source_target_pairs={{0,2},{1,3},{2,0},{3,1},{4,6},{5,7},{6,4},{7,5},{8,10},{9,11},{10,... | collective-permute-start | bytes 786440 | tf_op jit(solution)/shard_map/ppermute | solution.py:28
  99.7 12.8 %collective-permute-start = (bf16[2,1,128,512]{3,2,0,1:T(8,128)(2,1)S(1)}, bf16[2,1,128,512]{3,2,0,1:T(8,128)(2,1)S(1)}, u32[]{:S(2)}, u32[]{:S(2)}) collective-permute-start(bf16[2,1,128,512]{3,2,0,1:T(8,128)(2,1)S(1)} %get-tuple-element.12), channel_id=1, source_target_pairs={{0,1},{1,0},{2,3},{3,2},{4,5},{5,4},{6,7},{7,6},{8,9},{9,8},{10,11... | collective-permute-start | bytes 786440 | tf_op jit(solution)/shard_map/ppermute | solution.py:28
  169.6 33.4 %copy-start.5 = (f32[2,512,128]{1,2,0:T(8,128)S(1)}, f32[2,512,128]{1,2,0:T(8,128)}, u32[]{:S(2)}) copy-start(f32[2,512,128]{1,2,0:T(8,128)} %copy-done.4) | copy-start | bytes 1572868
  169.6 33.4 %copy-start.8 = (f32[2,256,128]{1,2,0:T(8,128)S(1)}, f32[2,256,128]{1,2,0:T(8,128)}, u32[]{:S(2)}) copy-start(f32[2,256,128]{1,2,0:T(8,128)} %copy-done.7) | copy-start | bytes 786436
  169.6 33.4 %copy-start.12 = (f32[2,128,128]{1,2,0:T(8,128)S(1)}, f32[2,128,128]{1,2,0:T(8,128)}, u32[]{:S(2)}) copy-start(f32[2,128,128]{1,2,0:T(8,128)} %copy-done.11) | copy-start | bytes 393220
  169.6 33.4 %copy-start.10 = (pred[512,512]{0,1:T(8,128)(4,1)S(1)}, pred[512,512]{0,1:T(8,128)(4,1)}, u32[]{:S(2)}) copy-start(pred[512,512]{0,1:T(8,128)(4,1)} %copy-done.9) | copy-start | bytes 786436
  203.0 1.9 copy-start.16
  204.9 1.2 copy-start.1
  204.9 1.5 copy-start.3
  (1 other events, 0.7 us)
Sparse Core Ops, SparseCore 0:
  19.6 74.4 reduce-scatter.1
Sparse Core Ops, SparseCore 1:
  22.3 151.2 all-gather.6
  175.1 33.8 all-gather.4
